TPU v7x, 32 devices: a whole 2x2x4 slice. The times are simulated.
32 devices in a mesh: dp: 8 (over y, x, core), mp: 4 (over z).
Axes of the slice: x: 2, y: 2, z: 4, core: 2. Of those that a mesh axis runs over, the one named last changes fastest.
Arguments:
- tokens: bfloat16 [17408, 1024], P(('dp', 'mp')), may hold values from -6 to 6
- groups: int32 [17408], P(('dp', 'mp')), may hold values from 0 to 15
- lengths: int32 [16], P('dp'), may hold values from 272 to 1088, as said below
- qkv_weight: bfloat16 [3, 1024, 1024], P(None, None, 'mp'), may hold values from -0.1875 to 0.1875
- qv_bias: bfloat16 [2, 1024], P(None, 'mp'), may hold values from -3 to 3
- out_weight: bfloat16 [1024, 1024], P('mp'), may hold values from -1.5 to 1.5
- out_bias: bfloat16 [1024], replicated, may hold values from -2 to 2
- up_weight: bfloat16 [1024, 4096], P(None, 'mp'), may hold values from -0.1875 to 0.1875
- up_bias: bfloat16 [4096], P('mp'), may hold values from -3 to 3
- down_weight: bfloat16 [4096, 1024], P('mp'), may hold values from -0.09375 to 0.09375
- down_bias: bfloat16 [1024], replicated, may hold values from -2 to 2
- norm_gain: bfloat16 [4, 1024], replicated, may hold values from 0.5 to 1.5
- norm_bias: bfloat16 [4, 1024], replicated, may hold values from -2 to 2
- group_table: bfloat16 [16, 1024], replicated, may hold values from -3 to 3
- cotangent: bfloat16 [17408, 1024], P(('dp', 'mp')), may hold values from -6 to 6
Outputs:
- output: bfloat16 [17408, 1024], P(('dp', 'mp'))
- input_grad: float32 [17408, 1024], P(('dp', 'mp'))
- qkv_grad: float32 [3, 1024, 1024], P(None, None, 'mp')
- qv_bias_grad: float32 [2, 1024], P(None, 'mp')
- out_weight_grad: float32 [1024, 1024], P('mp')
- out_bias_grad: float32 [1024], replicated
- up_weight_grad: float32 [1024, 4096], P(None, 'mp')
- up_bias_grad: float32 [4096], P('mp')
- down_weight_grad: float32 [4096, 1024], P('mp')
- down_bias_grad: float32 [1024], replicated
- norm_gain_grad: float32 [4, 1024], replicated
- norm_bias_grad: float32 [4, 1024], replicated
- group_table_grad: float32 [16, 1024], replicated
Inputs may be any that keep to these rules, and one draw needn't show every extreme that they name: `lengths`: each sequence's valid length; some sequence has all 1088 tokens valid and some only 272.
All inputs are finite; a program needn't handle non-finite values.
Results may differ from a plain program's by a relative error of at most 0.009.
Values may be sent and summed in bfloat16 or wider, within the bound.
No kernel may reach another device: no remote copies, remote signals or barrier semaphores. Data moves between devices by JAX's collectives and lax.ppermute only.
A program may use at most 192 MiB of HBM per device.

v0:
```python
import math
import jax
import jax.numpy as jnp
from jax import lax
from jax.sharding import PartitionSpec as P

HEAD_DIM = 64
SEQ_LEN = 1088
RELAX_ALPHA = 32.0
NORM_EPSILON = 1e-05
MASKED_SCORE = -1000000000.0
PRECISE = lax.Precision.HIGHEST


def norm_forward(inputs, gain_row, shift_row):
    centred = inputs - jnp.mean(inputs, axis=-1, keepdims=True)
    factor = lax.rsqrt(jnp.mean(centred * centred, axis=-1, keepdims=True) + NORM_EPSILON)
    normal = centred * factor
    return (normal * gain_row + shift_row, normal, factor)


def norm_backward(upstream, normal, factor, gain_row):
    scaled = upstream * gain_row
    adjusted = (
        scaled
        - jnp.mean(scaled, axis=-1, keepdims=True)
        - normal * jnp.mean(scaled * normal, axis=-1, keepdims=True)
    )
    return (adjusted * factor, jnp.sum(upstream * normal, axis=0), jnp.sum(upstream, axis=0))


def block_mask(block_index, block_rows, key_reach, length):
    row_ids = block_index * block_rows + lax.broadcasted_iota(jnp.int32, (block_rows, key_reach), 0)
    columns = lax.broadcasted_iota(jnp.int32, (block_rows, key_reach), 1)
    return (columns <= row_ids) & (columns < length)


def block_scores(queries, keys_seq, block_index, block_rows, length):
    key_reach = (block_index + 1) * block_rows
    first = block_index * block_rows
    scores = jnp.einsum(
        "qhd,khd->hqk",
        queries[first:key_reach],
        keys_seq[:key_reach],
        preferred_element_type=jnp.float32,
    )
    visible = block_mask(block_index, block_rows, key_reach, length)[None]
    return (jnp.where(visible, scores, MASKED_SCORE), visible)


def attend(inputs):
    queries, keys_seq, values_seq, length = inputs
    block_rows = queries.shape[0] // 2
    pieces = []
    log_sums = []
    for block_index in range(2):
        key_reach = (block_index + 1) * block_rows
        scores, visible = block_scores(queries, keys_seq, block_index, block_rows, length)
        row_top = jnp.max(scores, axis=-1, keepdims=True)
        exponent = jnp.exp((scores - row_top) * RELAX_ALPHA)
        row_total = jnp.sum(exponent, axis=-1, keepdims=True)
        probs_low = (exponent / row_total).astype(jnp.bfloat16)
        pieces.append(
            jnp.einsum(
                "hqk,khd->qhd",
                probs_low,
                values_seq[:key_reach],
                preferred_element_type=jnp.float32,
            )
        )
        log_sums.append((row_top * RELAX_ALPHA + jnp.log(row_total))[..., 0])
    return (jnp.concatenate(pieces, axis=0), jnp.concatenate(log_sums, axis=1))


def attend_back(inputs):
    queries, keys_seq, values_seq, length, log_sums, grad_out = inputs
    block_rows = queries.shape[0] // 2
    grad_keys = jnp.zeros(keys_seq.shape, jnp.float32)
    grad_values = jnp.zeros(values_seq.shape, jnp.float32)
    grad_pieces = []
    for block_index in range(2):
        key_reach = (block_index + 1) * block_rows
        first = block_index * block_rows
        scores, visible = block_scores(queries, keys_seq, block_index, block_rows, length)
        exact = jnp.where(
            visible, jnp.exp(scores * RELAX_ALPHA - log_sums[:, first:key_reach, None]), 0.0
        )
        grad_rows = grad_out[first:key_reach]
        grad_probs = jnp.einsum(
            "qhd,khd->hqk", grad_rows, values_seq[:key_reach], preferred_element_type=jnp.float32
        )
        grad_values = grad_values.at[:key_reach].add(
            jnp.einsum(
                "hqk,qhd->khd",
                exact.astype(jnp.bfloat16),
                grad_rows,
                preferred_element_type=jnp.float32,
            )
        )
        row_delta = jnp.sum(exact * grad_probs, axis=-1, keepdims=True)
        grad_scores = (exact * (grad_probs - row_delta) * RELAX_ALPHA).astype(jnp.bfloat16)
        grad_pieces.append(
            jnp.einsum(
                "hqk,khd->qhd",
                grad_scores,
                keys_seq[:key_reach],
                preferred_element_type=jnp.float32,
            )
        )
        grad_keys = grad_keys.at[:key_reach].add(
            jnp.einsum(
                "hqk,qhd->khd",
                grad_scores,
                queries[first:key_reach],
                preferred_element_type=jnp.float32,
            )
        )
    return (jnp.concatenate(grad_pieces, axis=0), grad_keys, grad_values)


def on_device(
    tokens,
    groups,
    lengths,
    qkv_weight,
    qv_bias,
    out_weight,
    out_bias,
    up_weight,
    up_bias,
    down_weight,
    down_bias,
    norm_gain,
    norm_bias,
    group_table,
    cotangent,
):
    gains = norm_gain.astype(jnp.float32)
    shifts = norm_bias.astype(jnp.float32)
    row_count = tokens.shape[0]
    onehot = (
        groups[:, None] == lax.broadcasted_iota(jnp.int32, (1, group_table.shape[0]), 1)
    ).astype(jnp.bfloat16)
    residual = tokens.astype(jnp.float32) + jnp.dot(
        onehot, group_table, preferred_element_type=jnp.float32
    )
    normed, norm_one, inv_one = norm_forward(residual, gains[0], shifts[0])
    normed_low = normed.astype(jnp.bfloat16)
    normed_all = lax.all_gather(normed_low, "mp", axis=0, tiled=True)
    projected = jnp.einsum(
        "td,cde->cte", normed_all, qkv_weight, preferred_element_type=jnp.float32
    )
    local_width = qkv_weight.shape[2]
    seq_count = lengths.shape[0]
    head_shape = (seq_count, SEQ_LEN, local_width // HEAD_DIM, HEAD_DIM)
    factor = 1.0 / (RELAX_ALPHA * math.sqrt(HEAD_DIM))
    biases = qv_bias.astype(jnp.float32)
    queries = ((projected[0] + biases[0]) * factor).astype(jnp.bfloat16).reshape(head_shape)
    keys_all = projected[1].astype(jnp.bfloat16).reshape(head_shape)
    values_all = (projected[2] + biases[1]).astype(jnp.bfloat16).reshape(head_shape)
    attended, log_sums = lax.map(attend, (queries, keys_all, values_all, lengths))
    attended_low = attended.reshape(seq_count * SEQ_LEN, local_width).astype(jnp.bfloat16)
    branch = lax.psum_scatter(
        jnp.dot(
            lax.slice_in_dim(attended_low, 0, row_count * lax.axis_size("mp"), axis=0),
            out_weight,
            preferred_element_type=jnp.float32,
        ),
        "mp",
        scatter_dimension=0,
        tiled=True,
    ) + out_bias.astype(jnp.float32)
    branch_out, norm_two, inv_two = norm_forward(branch, gains[1], shifts[1])
    middle = residual + branch_out
    mid_normed, norm_three, inv_three = norm_forward(middle, gains[2], shifts[2])
    mid_low = mid_normed.astype(jnp.bfloat16)
    mid_all = lax.all_gather(mid_low, "mp", axis=0, tiled=True)
    pre_act = jnp.dot(mid_all, up_weight, preferred_element_type=jnp.float32) + up_bias.astype(
        jnp.float32
    )
    activated, gelu_pull = jax.vjp(jax.nn.gelu, pre_act)
    activated_low = activated.astype(jnp.bfloat16)
    ffn_out = lax.psum_scatter(
        jnp.dot(
            lax.slice_in_dim(activated_low, 0, row_count * lax.axis_size("mp"), axis=0),
            down_weight,
            preferred_element_type=jnp.float32,
        ),
        "mp",
        scatter_dimension=0,
        tiled=True,
    ) + down_bias.astype(jnp.float32)
    ffn_normed, norm_four, inv_four = norm_forward(ffn_out, gains[3], shifts[3])
    output = (middle + ffn_normed).astype(jnp.bfloat16)
    upstream = cotangent.astype(jnp.float32)
    grad_ffn, gain_four, shift_four = norm_backward(upstream, norm_four, inv_four, gains[3])
    grad_ffn_low = grad_ffn.astype(jnp.bfloat16)
    down_bias_part = jnp.sum(grad_ffn_low.astype(jnp.float32), axis=0)
    grad_ffn_all = lax.all_gather(grad_ffn_low, "mp", axis=0, tiled=True)
    down_grad = jnp.dot(activated_low.T, grad_ffn_all, preferred_element_type=jnp.float32)
    grad_act = jnp.dot(grad_ffn_all, down_weight.T, preferred_element_type=jnp.float32)
    (grad_pre,) = gelu_pull(grad_act)
    grad_pre_low = grad_pre.astype(jnp.bfloat16)
    up_bias_grad = jnp.sum(grad_pre_low.astype(jnp.float32), axis=0)
    up_grad = jnp.dot(mid_all.T, grad_pre_low, preferred_element_type=jnp.float32)
    grad_mid = lax.psum_scatter(
        jnp.dot(
            lax.slice_in_dim(grad_pre_low, 0, row_count * lax.axis_size("mp"), axis=0),
            up_weight.T,
            preferred_element_type=jnp.float32,
        ),
        "mp",
        scatter_dimension=0,
        tiled=True,
    )
    back_three, gain_three, shift_three = norm_backward(grad_mid, norm_three, inv_three, gains[2])
    grad_middle = upstream + back_three
    grad_branch, gain_two, shift_two = norm_backward(grad_middle, norm_two, inv_two, gains[1])
    grad_branch_low = grad_branch.astype(jnp.bfloat16)
    out_bias_part = jnp.sum(grad_branch_low.astype(jnp.float32), axis=0)
    grad_branch_all = lax.all_gather(grad_branch_low, "mp", axis=0, tiled=True)
    out_grad = jnp.dot(attended_low.T, grad_branch_all, preferred_element_type=jnp.float32)
    grad_attended = (
        jnp.dot(grad_branch_all, out_weight.T, preferred_element_type=jnp.float32)
        .astype(jnp.bfloat16)
        .reshape(head_shape)
    )
    grad_queries, grad_keys, grad_values = lax.map(
        attend_back, (queries, keys_all, values_all, lengths, log_sums, grad_attended)
    )
    flat_shape = (seq_count * SEQ_LEN, local_width)
    grad_q_low = (grad_queries * factor).astype(jnp.bfloat16).reshape(flat_shape)
    grad_k_low = grad_keys.astype(jnp.bfloat16).reshape(flat_shape)
    grad_v_low = grad_values.astype(jnp.bfloat16).reshape(flat_shape)
    grad_projected = jnp.stack([grad_q_low, grad_k_low, grad_v_low])
    qv_bias_grad = jnp.stack(
        [
            jnp.sum(grad_q_low.astype(jnp.float32), axis=0),
            jnp.sum(grad_v_low.astype(jnp.float32), axis=0),
        ]
    )
    qkv_grad = jnp.einsum(
        "td,cte->cde", normed_all, grad_projected, preferred_element_type=jnp.float32
    )
    grad_normed = lax.psum_scatter(
        jnp.einsum(
            "cte,cde->td",
            lax.slice_in_dim(grad_projected, 0, row_count * lax.axis_size("mp"), axis=1),
            qkv_weight,
            preferred_element_type=jnp.float32,
        ).astype(jnp.bfloat16),
        "mp",
        scatter_dimension=0,
        tiled=True,
    ).astype(jnp.float32)
    back_one, gain_one, shift_one = norm_backward(grad_normed, norm_one, inv_one, gains[0])
    input_grad = grad_middle + back_one
    table_part = jnp.dot(
        onehot.astype(jnp.float32).T,
        input_grad,
        precision=PRECISE,
        preferred_element_type=jnp.float32,
    )
    gain_parts = jnp.stack([gain_one, gain_two, gain_three, gain_four])
    shift_parts = jnp.stack([shift_one, shift_two, shift_three, shift_four])
    qkv_grad, qv_bias_grad, out_grad, up_grad, up_bias_grad, down_grad = lax.psum(
        (qkv_grad, qv_bias_grad, out_grad, up_grad, up_bias_grad, down_grad), "dp"
    )
    gain_grad, shift_grad, out_bias_grad, down_bias_grad, table_grad = lax.psum(
        (gain_parts, shift_parts, out_bias_part, down_bias_part, table_part), ("dp", "mp")
    )
    return (
        output,
        input_grad,
        qkv_grad,
        qv_bias_grad,
        out_grad,
        out_bias_grad,
        up_grad,
        up_bias_grad,
        down_grad,
        down_bias_grad,
        gain_grad,
        shift_grad,
        table_grad,
    )


def solution(mesh):
    placed = (
        P(("dp", "mp"), None),
        P(("dp", "mp")),
        P("dp"),
        P(None, None, "mp"),
        P(None, "mp"),
        P("mp", None),
        P(),
        P(None, "mp"),
        P("mp"),
        P("mp", None),
        P(),
        P(),
        P(),
        P(),
        P(("dp", "mp"), None),
    )
    return jax.shard_map(
        on_device,
        mesh=mesh,
        in_specs=placed,
        out_specs=(
            P(("dp", "mp"), None),
            P(("dp", "mp"), None),
            P(None, None, "mp"),
            P(None, "mp"),
            P("mp", None),
            P(),
            P(None, "mp"),
            P("mp"),
            P("mp", None),
            P(),
            P(),
            P(),
            P(),
        ),
        check_vma=False,
    )
```

profile of v0, /device:TPU:1, one launch (start us, length us, event | category | flops | bytes accessed | tf_op | source)
XLA Modules:
  0.0 1619.4 jit_solution(17449451052311089601)
XLA Ops:
  15.2 87.1 %all-gather.5.cloned.1.call-done = bf16[2176,1024]{1,0:T(8,128)(2,1)} async-done(((bf16[544,1024]{1,0:T(8,128)(2,1)}), bf16[2176,1024]{1,0:T(8,128)(2,1)}) %all-gather.5.cloned.1.call-update) | async-done | bytes 4456464 | tf_op jit(solution)/shard_map/all_gather | solution.py:149
  102.3 5.9 convolution_bitcast_fusion
  123.6 4.6 copy.51
  139.2 39.9 %while.35 = (s32[]{:T(128)}, bf16[2,1088,4,64]{1,3,2,0:T(8,128)(2,1)S(1)}, f32[2,4,1088]{2,1,0:T(4,128)S(1)}, bf16[2,1088,4,64]{1,3,2,0:T(8,128)(2,1)}, s32[2]{0...) while((s32[]{:T(128)}, ...), condition=%wide.region_7.8_spmd, body=%wide.region_2.7_spmd.sunk | while | flops 951075200 | bytes 50647132 | solution.py:161
  154.5 4.3 fusion.216
  174.1 4.3 fusion.216
  184.3 6.2 fusion.156
  191.2 150.5 %reduce-scatter.5.cloned.1.call-done = f32[544,1024]{1,0:T(8,128)} async-done(((f32[2176,1024]{1,0:T(8,128)}), f32[544,1024]{1,0:T(8,128)}) %reduce-scatter.5.cloned.1.call-update) | async-done | bytes 2228240 | tf_op jit(solution)/shard_map/reduce_scatter | solution.py:163
  349.5 86.3 %all-gather.7.cloned.1.call-done = bf16[2176,1024]{1,0:T(8,128)(2,1)} async-done(((bf16[544,1024]{1,0:T(8,128)(2,1)}), bf16[2176,1024]{1,0:T(8,128)(2,1)}) %all-gather.7.cloned.1.call-update) | async-done | bytes 4456464 | tf_op jit(solution)/shard_map/all_gather | solution.py:177
  435.8 11.9 multiply_convert_fusion.2
  449.8 7.0 fusion.157
  457.5 150.5 %reduce-scatter.7.cloned.1.call-done = f32[544,1024]{1,0:T(8,128)} async-done(((f32[2176,1024]{1,0:T(8,128)}), f32[544,1024]{1,0:T(8,128)}) %reduce-scatter.7.cloned.1.call-update) | async-done | bytes 2228240 | tf_op jit(solution)/shard_map/reduce_scatter | solution.py:183
  615.6 86.3 %all-gather.9.cloned.1.call-done = bf16[2176,1024]{1,0:T(8,128)(2,1)} async-done(((bf16[544,1024]{1,0:T(8,128)(2,1)}), bf16[2176,1024]{1,0:T(8,128)(2,1)}) %all-gather.9.cloned.1.call-update) | async-done | bytes 4456464 | tf_op jit(solution)/shard_map/all_gather | solution.py:199
  701.9 15.1 convert_reduce_fusion
  719.0 7.2 fusion.158
  726.7 150.8 %reduce-scatter.9.cloned.1.call-done = f32[544,1024]{1,0:T(8,128)} async-done(((f32[2176,1024]{1,0:T(8,128)}), f32[544,1024]{1,0:T(8,128)}) %reduce-scatter.9.cloned.1.call-update) | async-done | bytes 2228240 | tf_op jit(solution)/shard_map/reduce_scatter | solution.py:206
  881.5 5.1 multiply_reduce_fusion.3
  889.1 9.7 fusion.161
  898.9 9.3 fusion.160
  908.1 67.3 %all-gather.11.cloned.1.call-done = bf16[2176,1024]{1,0:T(8,128)(2,1)} async-done(((bf16[544,1024]{1,0:T(8,128)(2,1)}), bf16[2176,1024]{1,0:T(8,128)(2,1)}) %all-gather.11.cloned.1.call-update) | async-done | bytes 4456464 | tf_op jit(solution)/shard_map/all_gather | solution.py:221
  987.1 199.1 %while.36 = (s32[]{:T(128)}, f32[2,1088,4,64]{1,0,3,2:T(2,128)}, bf16[2,1088,4,64]{1,3,2,0:T(8,128)(2,1)}, bf16[2,1088,4,64]{1,3,2,0:T(8,128)(2,1)}, bf16[2,1088...) while((s32[]{:T(128)}, f32[2,1088,4,64]{1,0,3,2:T(2,128)}, ...), condition=%wide.region_26.27_spmd, body=%wide.region_23.26_spmd.sunk | while | flops 2328682240 | bytes 256355056 | solution.py:228
  995.1 4.4 fusion.236
  999.5 9.9 fusion.238
  1009.4 9.1 fusion.237
  1018.5 4.9 exponential_select_fusion.4
  1028.3 6.5 fusion.233
  1034.8 15.7 fusion.239
  1050.5 15.0 fusion.234
  1066.9 19.6 %dynamic_update_slice.42 = f32[2,1088,4,64]{1,0,3,2:T(2,128)} dynamic-update-slice(f32[2,1088,4,64]{1,0,3,2:T(2,128)} %get-tuple-element.608, f32[1,1088,4,64]{1,0,3,2:T(1,128)S(1)} %copy.111, s32[]{:T(128)S(6)} %copy.130, s32[]{:T(128)} %constant.238.clone.1..sunk.1, s32[]{:T(128)} %constant.238.clone.1..sunk.1, s32[]{:T(128)} %constant.238.clone.1..sunk.1) | dynamic-update-slice | bytes 2228228 | tf_op jit(solution)/shard_map/while/body/jit(dynamic_update_index_in_dim)/dynamic_update_slice | solution.py:161
  1094.5 4.4 fusion.236
  1098.9 9.9 fusion.238
  1108.8 9.1 fusion.237
  1117.8 4.9 exponential_select_fusion.4
  1127.7 6.5 fusion.233
  1134.2 15.8 fusion.239
  1149.9 14.9 fusion.234
  1166.3 19.6 %dynamic_update_slice.42 = f32[2,1088,4,64]{1,0,3,2:T(2,128)} dynamic-update-slice(f32[2,1088,4,64]{1,0,3,2:T(2,128)} %get-tuple-element.608, f32[1,1088,4,64]{1,0,3,2:T(1,128)S(1)} %copy.111, s32[]{:T(128)S(6)} %copy.130, s32[]{:T(128)} %constant.238.clone.1..sunk.1, s32[]{:T(128)} %constant.238.clone.1..sunk.1, s32[]{:T(128)} %constant.238.clone.1..sunk.1) | dynamic-update-slice | bytes 2228228 | tf_op jit(solution)/shard_map/while/body/jit(dynamic_update_index_in_dim)/dynamic_update_slice | solution.py:161
  1192.7 4.4 reshape.437
  1204.3 4.5 reshape.436
  1208.8 4.8 fusion.159
  1213.6 5.6 fusion.140
  1220.5 7.8 bitcast_convert_fusion
  1228.9 13.3 all-reduce.3
  1242.2 149.4 %all-reduce.10.cloned.1.call-done = (f32[3,1024,256]{1,2,0:T(8,128)}, f32[256,1024]{1,0:T(8,128)}, f32[1024,1024]{1,0:T(8,128)}, f32[1024,1024]{1,0:T(8,128)}) async-done(((f32[3,1024,256]{1,2,0:T(8,128)}, f32[256,1024]{1,0:T(8,128)}, f32[1024,1024]{1,0:T(8,128)}, f32[1024,1024]{1,0:T(8,128)}), (f32[3,1024,256]{1,2,0:T(8,128)}, f32[256,1024]{1,0:T(8,128)}, f32[1024,1024]{1,0:T(8,128)}, ...) | async-done | bytes 12582928 | tf_op jit(solution)/shard_map/psum | solution.py:266
  1395.1 80.2 %reduce-scatter.11.cloned.1.call-done = bf16[544,1024]{1,0:T(8,128)(2,1)} async-done(((bf16[2176,1024]{1,0:T(8,128)(2,1)}), bf16[544,1024]{1,0:T(8,128)(2,1)}) %reduce-scatter.11.cloned.1.call-update) | async-done | bytes 1114128 | tf_op jit(solution)/shard_map/reduce_scatter | solution.py:245
  1484.1 41.4 %all-reduce.2 = (f32[1024]{0:T(1024)}, f32[1024]{0:T(1024)}, f32[4,1024]{1,0:T(4,128)}, f32[4,1024]{1,0:T(4,128)}) all-reduce(f32[1024]{0:T(1024)S(1)} %copy-done.42, f32[1024]{0:T(1024)S(1)} %copy-done.41, f32[4,1024]{1,0:T(4,128)S(1)} %pad_maximum_fusion.3, ...), channel_id=1, replica_groups=mesh['dp'=8,'mp'=4] {'dp','mp'}, use_global_device_ids=true, to_apply=%region_36.37 | all-reduce | flops 10240 | bytes 81920 | tf_op jit(solution)/shard_map/psum | solution.py:269
  1525.4 78.4 %all-reduce.8.cloned.1.call-done = f32[16,1024]{1,0:T(8,128)} async-done(((f32[16,1024]{1,0:T(8,128)}), f32[16,1024]{1,0:T(8,128)}) %all-reduce.8.cloned.1.call-update) | async-done | bytes 65552 | tf_op jit(solution)/shard_map/psum | solution.py:269
  1604.8 4.9 copy.144
  (292 shorter events, 168.7 us)
Async XLA Ops:
  7.2 428.6 %copy-start = (bf16[1024,1024]{1,0:T(8,128)(2,1)S(1)}, bf16[1024,1024]{1,0:T(8,128)(2,1)}, u32[]{:S(2)}) copy-start(bf16[1024,1024]{1,0:T(8,128)(2,1)} %param.38) | copy-start | bytes 6291460
  7.2 95.1 %all-gather.5.cloned.1.call-start = ((), (), s32[]{:S(2)}) async-start(), calls=%async_computation.4 | async-start | bytes 5570560 | tf_op jit(solution)/shard_map/all_gather | solution.py:149
  8.7 3.8 copy-start.34
  14.9 326.8 %reduce-scatter.5.cloned.1.call-start = ((), (), s32[]{:S(2)}) async-start(), calls=%async_computation.5 | async-start | bytes 11141120 | tf_op jit(solution)/shard_map/reduce_scatter | solution.py:163
  184.3 6.2 copy-start.19
  190.5 245.3 %all-gather.7.cloned.1.call-start = ((), (), s32[]{:S(2)}) async-start(), calls=%async_computation.6 | async-start | bytes 5570560 | tf_op jit(solution)/shard_map/all_gather | solution.py:177
  191.2 154.6 %copy-start.36 = (f32[1,1024]{1,0:T(1,128)S(1)}, f32[1,1024]{1,0:T(1,128)}, u32[]{:S(2)}) copy-start(f32[1,1024]{1,0:T(1,128)} %get-tuple-element.433) | copy-start | bytes 12292
  191.2 154.6 %copy-start.51 = (f32[1,1024]{1,0:T(1,128)S(1)}, f32[1,1024]{1,0:T(1,128)}, u32[]{:S(2)}) copy-start(f32[1,1024]{1,0:T(1,128)} %get-tuple-element.437) | copy-start | bytes 12292
  341.7 4.1 copy-start.5
  341.7 4.1 copy-start.9
  349.4 258.6 %reduce-scatter.7.cloned.1.call-start = ((), (), s32[]{:S(2)}) async-start(), calls=%async_computation.7 | async-start | bytes 11141120 | tf_op jit(solution)/shard_map/reduce_scatter | solution.py:183
  435.8 14.0 copy-start.58
  456.9 245.0 %all-gather.9.cloned.1.call-start = ((), (), s32[]{:S(2)}) async-start(), calls=%async_computation.8 | async-start | bytes 5570560 | tf_op jit(solution)/shard_map/all_gather | solution.py:199
  457.5 153.3 %copy-start.39 = (f32[1,1024]{1,0:T(1,128)S(1)}, f32[1,1024]{1,0:T(1,128)}, u32[]{:S(2)}) copy-start(f32[1,1024]{1,0:T(1,128)} %get-tuple-element.431) | copy-start | bytes 12292
  608.1 2.8 copy-start.16
  615.5 261.9 %reduce-scatter.9.cloned.1.call-start = ((), (), s32[]{:S(2)}) async-start(), calls=%async_computation.9 | async-start | bytes 11141120 | tf_op jit(solution)/shard_map/reduce_scatter | solution.py:206
  726.3 249.2 %all-gather.11.cloned.1.call-start = ((), (), s32[]{:S(2)}) async-start(), calls=%async_computation.10 | async-start | bytes 5570560 | tf_op jit(solution)/shard_map/all_gather | solution.py:221
  877.5 4.0 copy-start.18
  881.5 5.2 copy-start.10
  886.6 2.4 copy-start.12
  886.6 12.2 slice-start
  889.1 502.5 %all-reduce.10.cloned.1.call-start = ((), (), s32[]{:S(2)}) async-start(), calls=%async_computation.13 | async-start | bytes 25165824 | tf_op jit(solution)/shard_map/psum | solution.py:266
  889.1 9.7 slice-start.1
  898.9 76.6 %copy-start.29 = (bf16[256,1024]{1,0:T(8,128)(2,1)S(1)}, bf16[256,1024]{1,0:T(8,128)(2,1)}, u32[]{:S(2)}) copy-start(bf16[256,1024]{1,0:T(8,128)(2,1)} %param.36) | copy-start | bytes 1572868
  1018.5 5.0 copy-start.13
  1023.5 3.8 copy-start.2
  1028.3 6.5 copy-start.62
  1117.8 5.0 copy-start.13
  1122.8 3.8 copy-start.2
  1127.7 6.5 copy-start.62
  1186.2 3.4 copy-start.15
  1198.7 2.5 copy-start.21
  1204.3 4.5 copy-start.20
  1208.7 4.8 copy-start.24
  1208.8 4.8 copy-start.26
  1208.8 4.8 copy-start.27
  1208.8 4.8 copy-start.57
  1219.2 256.1 %reduce-scatter.11.cloned.1.call-start = ((), (), s32[]{:S(2)}) async-start(), calls=%async_computation.11 | async-start | bytes 5570560 | tf_op jit(solution)/shard_map/reduce_scatter | solution.py:245
  1228.3 375.6 %all-reduce.8.cloned.1.call-start = ((), (), s32[]{:S(2)}) async-start(), calls=%async_computation.12 | async-start | bytes 131072 | tf_op jit(solution)/shard_map/psum | solution.py:269
  1391.6 83.7 %copy-start.31 = (f32[544]{0:T(1024)S(1)}, f32[544]{0:T(1024)}, u32[]{:S(2)}) copy-start(f32[544]{0:T(1024)} %copy-done.30) | copy-start | bytes 6532
  1391.6 83.7 %copy-start.33 = (f32[544]{0:T(1024)S(1)}, f32[544]{0:T(1024)}, u32[]{:S(2)}) copy-start(f32[544]{0:T(1024)} %copy-done.32) | copy-start | bytes 6532
  1391.6 83.7 %copy-start.35 = (f32[1,1024]{1,0:T(1,128)S(1)}, f32[1,1024]{1,0:T(1,128)}, u32[]{:S(2)}) copy-start(f32[1,1024]{1,0:T(1,128)} %copy-done.34) | copy-start | bytes 12292
  1475.3 3.2 copy-start.6
  1475.3 3.2 copy-start.22
  1478.5 3.8 copy-start.40
  1482.4 121.5 %copy-start.28 = (f32[256,1024]{1,0:T(8,128)S(1)}, f32[256,1024]{1,0:T(8,128)}, u32[]{:S(2)}) copy-start(f32[256,1024]{1,0:T(8,128)} %get-tuple-element.637) | copy-start | bytes 3145732
  1604.8 4.9 copy-start.23
  1604.8 7.6 copy-start.1
  (32 other events, 49.1 us)
Sparse Core Ops, SparseCore 0:
  15.0 87.1 all-gather.4
  190.6 151.0 reduce-scatter.4
  349.5 86.1 all-gather.6
  457.0 151.0 reduce-scatter.6
  615.6 86.1 all-gather.8
  726.4 151.0 reduce-scatter.8
  889.2 86.1 all-gather.10
  1219.4 172.1 all-reduce.9
  1394.0 81.2 reduce-scatter.10
  1484.1 119.7 all-reduce.7
where the time goes:
time: 1630 us; the launch traced here: 1620 us
  waiting for transfers between devices  1090 us (67%)
  matrix products  263 us (16%)
  local copies, waits for them, and re-layouts  138 us (8%)
  other arithmetic  59.1 us (4%)
  blocking collectives  54.6 us (3%)
    reduce_scatter x1, waiting for transfers between devices, on_device(): lax.psum_scatter(jnp.dot(lax.slice_in_dim(grad_pre_low, 0, row_count * la...  151 us
    reduce_scatter x1, waiting for transfers between devices, on_device(): lax.psum_scatter(jnp.dot(lax.slice_in_dim(activated_low, 0, row_count * l...  151 us
    reduce_scatter x1, waiting for transfers between devices, on_device(): lax.psum_scatter(jnp.dot(lax.slice_in_dim(attended_low, 0, row_count * la...  151 us
    psum x1, waiting for transfers between devices, on_device(): lax.psum((qkv_grad, qv_bias_grad, out_grad, up_grad, up_bias_grad, down_g...  149 us
    all_gather x1, waiting for transfers between devices, on_device(): normed_all = lax.all_gather(normed_low, 'mp', axis=0, tiled=True)  87.1 us
    all_gather x1, waiting for transfers between devices, on_device(): grad_ffn_all = lax.all_gather(grad_ffn_low, 'mp', axis=0, tiled=True)  86.3 us
    all_gather x1, waiting for transfers between devices, on_device(): mid_all = lax.all_gather(mid_low, 'mp', axis=0, tiled=True)  86.3 us
    reduce_scatter x1, waiting for transfers between devices, on_device(): lax.psum_scatter(jnp.einsum('cte,cde->td', lax.slice_in_dim(grad_projecte...  80.2 us
  transfers between devices with their start and end apart: 10, of which 10 were waited for; matrix products, arithmetic and copies ran while one was open for 2% of the time, Pallas kernels for 0%

commit v1 on v0

--- a/solution.py
+++ b/solution.py
@@ -10,6 +10,12 @@
 NORM_EPSILON = 1e-05
 MASKED_SCORE = -1000000000.0
 PRECISE = lax.Precision.HIGHEST
+
+
+def time_point_here(values, axis_name, row_axis):
+    for c in (axis_name, row_axis):
+        values = lax.psum(values, c)
+    return values
 
 
 def norm_forward(inputs, gain_row, shift_row):
@@ -266,8 +272,8 @@
     qkv_grad, qv_bias_grad, out_grad, up_grad, up_bias_grad, down_grad = lax.psum(
         (qkv_grad, qv_bias_grad, out_grad, up_grad, up_bias_grad, down_grad), "dp"
     )
-    gain_grad, shift_grad, out_bias_grad, down_bias_grad, table_grad = lax.psum(
-        (gain_parts, shift_parts, out_bias_part, down_bias_part, table_part), ("dp", "mp")
+    gain_grad, shift_grad, out_bias_grad, down_bias_grad, table_grad = time_point_here(
+        (gain_parts, shift_parts, out_bias_part, down_bias_part, table_part), "mp", "dp"
     )
     return (
         output,

time: 1630 us -> 1550 us (0.951)
  waiting for transfers between devices: 1090 us -> 1020 us
    psum x1, waiting for transfers between devices: 78.4 us -> 28 us  [time_point_here(): values = lax.psum(values, c)]
    psum x1, blocking collectives: 41.4 us -> 14.9 us  [time_point_here(): values = lax.psum(values, c)]
    reduce_scatter x1, waiting for transfers between devices: 80.2 us -> 54.3 us  [on_device(): lax.psum_scatter(jnp.einsum('cte,cde->td', lax.slice_in_dim(grad_projecte...]
    all_gather x1, waiting for transfers between devices: 67.3 us -> 86.3 us  [on_device(): grad_branch_all = lax.all_gather(grad_branch_low, 'mp', axis=0, tiled=True)]
where the time goes in v1:
time: 1550 us; the launch traced here: 1540 us
  waiting for transfers between devices  1020 us (66%)
  matrix products  264 us (17%)
  local copies, waits for them, and re-layouts  137 us (9%)
  other arithmetic  59.1 us (4%)
  blocking collectives  44.4 us (3%)
    reduce_scatter x1, waiting for transfers between devices, on_device(): lax.psum_scatter(jnp.dot(lax.slice_in_dim(grad_pre_low, 0, row_count * la...  151 us
    reduce_scatter x1, waiting for transfers between devices, on_device(): lax.psum_scatter(jnp.dot(lax.slice_in_dim(activated_low, 0, row_count * l...  151 us
    reduce_scatter x1, waiting for transfers between devices, on_device(): lax.psum_scatter(jnp.dot(lax.slice_in_dim(attended_low, 0, row_count * la...  151 us
    psum x1, waiting for transfers between devices, on_device(): lax.psum((qkv_grad, qv_bias_grad, out_grad, up_grad, up_bias_grad, down_g...  139 us
    all_gather x1, waiting for transfers between devices, on_device(): normed_all = lax.all_gather(normed_low, 'mp', axis=0, tiled=True)  87.1 us
    all_gather x1, waiting for transfers between devices, on_device(): grad_ffn_all = lax.all_gather(grad_ffn_low, 'mp', axis=0, tiled=True)  86.3 us
    all_gather x1, waiting for transfers between devices, on_device(): grad_branch_all = lax.all_gather(grad_branch_low, 'mp', axis=0, tiled=True)  86.3 us
    all_gather x1, waiting for transfers between devices, on_device(): mid_all = lax.all_gather(mid_low, 'mp', axis=0, tiled=True)  86.3 us
  transfers between devices with their start and end apart: 10, of which 10 were waited for; matrix products, arithmetic and copies ran while one was open for 2% of the time, Pallas kernels for 0%

profile of v1, /device:TPU:1, one launch (start us, length us, event | category | flops | bytes accessed | tf_op | source)
XLA Modules:
  0.0 1540.4 jit_solution(2936672181389591621)
XLA Ops:
  15.2 87.1 %all-gather.5.cloned.1.call-done = bf16[2176,1024]{1,0:T(8,128)(2,1)} async-done(((bf16[544,1024]{1,0:T(8,128)(2,1)}), bf16[2176,1024]{1,0:T(8,128)(2,1)}) %all-gather.5.cloned.1.call-update) | async-done | bytes 4456464 | tf_op jit(solution)/shard_map/all_gather | solution.py:155
  102.3 5.9 convolution_bitcast_fusion
  123.6 4.6 copy.51
  139.1 39.8 %while.35 = (s32[]{:T(128)}, bf16[2,1088,4,64]{1,3,2,0:T(8,128)(2,1)S(1)}, f32[2,4,1088]{2,1,0:T(4,128)S(1)}, bf16[2,1088,4,64]{1,3,2,0:T(8,128)(2,1)}, s32[2]{0...) while((s32[]{:T(128)}, ...), condition=%wide.region_7.8_spmd, body=%wide.region_2.7_spmd.sunk | while | flops 951075200 | bytes 50647132 | solution.py:167
  154.3 4.3 fusion.216
  173.9 4.3 fusion.216
  184.1 6.2 fusion.156
  191.0 150.5 %reduce-scatter.5.cloned.1.call-done = f32[544,1024]{1,0:T(8,128)} async-done(((f32[2176,1024]{1,0:T(8,128)}), f32[544,1024]{1,0:T(8,128)}) %reduce-scatter.5.cloned.1.call-update) | async-done | bytes 2228240 | tf_op jit(solution)/shard_map/reduce_scatter | solution.py:169
  349.3 86.3 %all-gather.7.cloned.1.call-done = bf16[2176,1024]{1,0:T(8,128)(2,1)} async-done(((bf16[544,1024]{1,0:T(8,128)(2,1)}), bf16[2176,1024]{1,0:T(8,128)(2,1)}) %all-gather.7.cloned.1.call-update) | async-done | bytes 4456464 | tf_op jit(solution)/shard_map/all_gather | solution.py:183
  435.6 11.9 multiply_convert_fusion.2
  449.5 7.0 fusion.157
  457.2 150.6 %reduce-scatter.7.cloned.1.call-done = f32[544,1024]{1,0:T(8,128)} async-done(((f32[2176,1024]{1,0:T(8,128)}), f32[544,1024]{1,0:T(8,128)}) %reduce-scatter.7.cloned.1.call-update) | async-done | bytes 2228240 | tf_op jit(solution)/shard_map/reduce_scatter | solution.py:189
  615.3 86.3 %all-gather.9.cloned.1.call-done = bf16[2176,1024]{1,0:T(8,128)(2,1)} async-done(((bf16[544,1024]{1,0:T(8,128)(2,1)}), bf16[2176,1024]{1,0:T(8,128)(2,1)}) %all-gather.9.cloned.1.call-update) | async-done | bytes 4456464 | tf_op jit(solution)/shard_map/all_gather | solution.py:205
  701.6 15.1 convert_reduce_fusion
  718.7 7.2 fusion.158
  726.0 151.2 %reduce-scatter.9.cloned.1.call-done = f32[544,1024]{1,0:T(8,128)} async-done(((f32[2176,1024]{1,0:T(8,128)}), f32[544,1024]{1,0:T(8,128)}) %reduce-scatter.9.cloned.1.call-update) | async-done | bytes 2228240 | tf_op jit(solution)/shard_map/reduce_scatter | solution.py:212
  881.2 5.1 multiply_reduce_fusion.3
  888.8 86.3 %all-gather.11.cloned.1.call-done = bf16[2176,1024]{1,0:T(8,128)(2,1)} async-done(((bf16[544,1024]{1,0:T(8,128)(2,1)}), bf16[2176,1024]{1,0:T(8,128)(2,1)}) %all-gather.11.cloned.1.call-update) | async-done | bytes 4456464 | tf_op jit(solution)/shard_map/all_gather | solution.py:227
  986.7 199.2 %while.36 = (s32[]{:T(128)}, f32[2,1088,4,64]{1,0,3,2:T(2,128)}, bf16[2,1088,4,64]{1,3,2,0:T(8,128)(2,1)}, bf16[2,1088,4,64]{1,3,2,0:T(8,128)(2,1)}, bf16[2,1088...) while((s32[]{:T(128)}, f32[2,1088,4,64]{1,0,3,2:T(2,128)}, ...), condition=%wide.region_26.27_spmd, body=%wide.region_23.26_spmd.sunk | while | flops 2328682240 | bytes 256355056 | solution.py:234
  995.0 4.4 fusion.236
  999.4 9.9 fusion.238
  1009.3 9.0 fusion.237
  1018.3 4.9 exponential_select_fusion.4
  1028.2 6.5 fusion.233
  1034.7 15.7 %fusion.239 = bf16[2,1088,4,64]{1,3,2,0:T(8,128)(2,1)} fusion(bf16[2,1088,4,64]{1,3,2,0:T(8,128)(2,1)} %get-tuple-element.614, s32[]{:T(128)S(6)} %copy.130, f32[4,544,1088]{2,1,0:T(8,128)} %copy-done.2, f32[4,544,1088]{2,1,0:T(8,128)} %fusion.233, f32[544,4,64]{0,2,1:T(8,128)S(1)} %copy-done.60, bf16[2,1088,4,64]{1,3,2,0:T(8,128)(2,1)} %get-tuple-element.631, ...), kind=kOutput, calls=%fused_computation.66.clone.1 | convolution fusion | flops 315157696 | bytes 42108416 | tf_op jit(solution)/shard_map/while/body/eval_jaxpr/hqk,qhd->khd/dot_general | solution.py:117
  1050.4 14.9 fusion.234
  1066.8 19.6 %dynamic_update_slice.42 = f32[2,1088,4,64]{1,0,3,2:T(2,128)} dynamic-update-slice(f32[2,1088,4,64]{1,0,3,2:T(2,128)} %get-tuple-element.613, f32[1,1088,4,64]{1,0,3,2:T(1,128)S(1)} %copy.111, s32[]{:T(128)S(6)} %copy.130, s32[]{:T(128)} %constant.238.clone.1..sunk.1, s32[]{:T(128)} %constant.238.clone.1..sunk.1, s32[]{:T(128)} %constant.238.clone.1..sunk.1) | dynamic-update-slice | bytes 2228228 | tf_op jit(solution)/shard_map/while/body/jit(dynamic_update_index_in_dim)/dynamic_update_slice | solution.py:167
  1094.4 4.4 fusion.236
  1098.7 9.9 fusion.238
  1108.7 9.0 fusion.237
  1117.7 4.9 exponential_select_fusion.4
  1127.6 6.5 fusion.233
  1134.1 15.7 %fusion.239 = bf16[2,1088,4,64]{1,3,2,0:T(8,128)(2,1)} fusion(bf16[2,1088,4,64]{1,3,2,0:T(8,128)(2,1)} %get-tuple-element.614, s32[]{:T(128)S(6)} %copy.130, f32[4,544,1088]{2,1,0:T(8,128)} %copy-done.2, f32[4,544,1088]{2,1,0:T(8,128)} %fusion.233, f32[544,4,64]{0,2,1:T(8,128)S(1)} %copy-done.60, bf16[2,1088,4,64]{1,3,2,0:T(8,128)(2,1)} %get-tuple-element.631, ...), kind=kOutput, calls=%fused_computation.66.clone.1 | convolution fusion | flops 315157696 | bytes 42108416 | tf_op jit(solution)/shard_map/while/body/eval_jaxpr/hqk,qhd->khd/dot_general | solution.py:117
  1149.8 15.0 fusion.234
  1166.2 19.6 %dynamic_update_slice.42 = f32[2,1088,4,64]{1,0,3,2:T(2,128)} dynamic-update-slice(f32[2,1088,4,64]{1,0,3,2:T(2,128)} %get-tuple-element.613, f32[1,1088,4,64]{1,0,3,2:T(1,128)S(1)} %copy.111, s32[]{:T(128)S(6)} %copy.130, s32[]{:T(128)} %constant.238.clone.1..sunk.1, s32[]{:T(128)} %constant.238.clone.1..sunk.1, s32[]{:T(128)} %constant.238.clone.1..sunk.1) | dynamic-update-slice | bytes 2228228 | tf_op jit(solution)/shard_map/while/body/jit(dynamic_update_index_in_dim)/dynamic_update_slice | solution.py:167
  1192.5 4.4 reshape.437
  1204.1 4.5 reshape.436
  1208.6 7.8 bitcast_convert_fusion
  1216.4 9.9 fusion.161
  1226.4 9.7 fusion.160
  1236.1 5.6 fusion.140
  1241.8 54.3 %reduce-scatter.11.cloned.1.call-done = bf16[544,1024]{1,0:T(8,128)(2,1)} async-done(((bf16[2176,1024]{1,0:T(8,128)(2,1)}), bf16[544,1024]{1,0:T(8,128)(2,1)}) %reduce-scatter.11.cloned.1.call-update) | async-done | bytes 1114128 | tf_op jit(solution)/shard_map/reduce_scatter | solution.py:251
  1304.7 4.6 fusion.159
  1309.3 28.0 %all-reduce.8.cloned.1.call-done = f32[16,1024]{1,0:T(8,128)} async-done(((f32[16,1024]{1,0:T(8,128)}), f32[16,1024]{1,0:T(8,128)}) %all-reduce.8.cloned.1.call-update) | async-done | bytes 65552 | tf_op jit(solution)/shard_map/psum | solution.py:17
  1338.1 14.9 all-reduce.4
  1353.0 29.5 %all-reduce.2 = (f32[2,256]{1,0:T(2,128)}, f32[1024]{0:T(1024)}, f32[1024]{0:T(1024)}, f32[1024]{0:T(1024)}, f32[4,1024]{1,0:T(4,128)}, /*index=5*/f32[4,1024]{1,0:T(4,128)}) all-reduce(f32[2,256]{1,0:T(2,128)S(1)} %pad_maximum_fusion.5, f32[1024]{0:T(1024)S(1)} %get-tuple-element.409, ...), channel_id=1, replica_groups=mesh['dp'=8,'mp'=4] {'dp'}, use_global_device_ids=true, to_apply=%region_33.34 | all-reduce | flops 11776 | bytes 94208 | tf_op jit(solution)/shard_map/psum | solution.py:272
  1382.5 138.6 %all-reduce.10.cloned.1.call-done = (f32[3,1024,256]{1,2,0:T(8,128)}, f32[256,1024]{1,0:T(8,128)}, f32[1024,1024]{1,0:T(8,128)}, f32[1024,1024]{1,0:T(8,128)}, f32[16,1024]{1,0:T(8,128)}) async-done(((f32[3,1024,256]{1,2,0:T(8,128)}, f32[256,1024]{1,0:T(8,128)}, f32[1024,1024]{1,0:T(8,128)}, f32[1024,1024]{1,0:T(8,128)}, f32[16,1024]{1,0:T(8,128)}), (f32[3,1024,256]{1,2,0:T(8,128)}, f32[256,1024]{1,0:T(8,128)}, ...) | async-done | bytes 12648464 | tf_op jit(solution)/shard_map/psum | solution.py:272
  1525.7 4.9 copy.145
  (288 shorter events, 167.1 us)
Async XLA Ops:
  7.2 428.4 %copy-start = (bf16[1024,1024]{1,0:T(8,128)(2,1)S(1)}, bf16[1024,1024]{1,0:T(8,128)(2,1)}, u32[]{:S(2)}) copy-start(bf16[1024,1024]{1,0:T(8,128)(2,1)} %param.38) | copy-start | bytes 6291460
  7.2 95.1 %all-gather.5.cloned.1.call-start = ((), (), s32[]{:S(2)}) async-start(), calls=%async_computation.4 | async-start | bytes 5570560 | tf_op jit(solution)/shard_map/all_gather | solution.py:155
  8.7 3.8 copy-start.33
  14.9 326.6 %reduce-scatter.5.cloned.1.call-start = ((), (), s32[]{:S(2)}) async-start(), calls=%async_computation.5 | async-start | bytes 11141120 | tf_op jit(solution)/shard_map/reduce_scatter | solution.py:169
  184.1 6.2 copy-start.19
  190.3 245.3 %all-gather.7.cloned.1.call-start = ((), (), s32[]{:S(2)}) async-start(), calls=%async_computation.6 | async-start | bytes 5570560 | tf_op jit(solution)/shard_map/all_gather | solution.py:183
  191.0 154.6 %copy-start.35 = (f32[1,1024]{1,0:T(1,128)S(1)}, f32[1,1024]{1,0:T(1,128)}, u32[]{:S(2)}) copy-start(f32[1,1024]{1,0:T(1,128)} %get-tuple-element.438) | copy-start | bytes 12292
  191.0 154.7 %copy-start.50 = (f32[1,1024]{1,0:T(1,128)S(1)}, f32[1,1024]{1,0:T(1,128)}, u32[]{:S(2)}) copy-start(f32[1,1024]{1,0:T(1,128)} %get-tuple-element.442) | copy-start | bytes 12292
  341.5 4.1 copy-start.5
  341.5 4.1 copy-start.9
  349.2 258.5 %reduce-scatter.7.cloned.1.call-start = ((), (), s32[]{:S(2)}) async-start(), calls=%async_computation.7 | async-start | bytes 11141120 | tf_op jit(solution)/shard_map/reduce_scatter | solution.py:189
  435.6 13.9 copy-start.56
  456.5 245.0 %all-gather.9.cloned.1.call-start = ((), (), s32[]{:S(2)}) async-start(), calls=%async_computation.8 | async-start | bytes 5570560 | tf_op jit(solution)/shard_map/all_gather | solution.py:205
  457.2 153.3 %copy-start.38 = (f32[1,1024]{1,0:T(1,128)S(1)}, f32[1,1024]{1,0:T(1,128)}, u32[]{:S(2)}) copy-start(f32[1,1024]{1,0:T(1,128)} %get-tuple-element.436) | copy-start | bytes 12292
  607.8 2.8 copy-start.16
  615.2 262.0 %reduce-scatter.9.cloned.1.call-start = ((), (), s32[]{:S(2)}) async-start(), calls=%async_computation.9 | async-start | bytes 11141120 | tf_op jit(solution)/shard_map/reduce_scatter | solution.py:212
  726.0 249.1 %all-gather.11.cloned.1.call-start = ((), (), s32[]{:S(2)}) async-start(), calls=%async_computation.10 | async-start | bytes 5570560 | tf_op jit(solution)/shard_map/all_gather | solution.py:227
  877.2 4.0 copy-start.18
  881.2 5.2 copy-start.10
  886.3 88.8 %copy-start.28 = (bf16[256,1024]{1,0:T(8,128)(2,1)S(1)}, bf16[256,1024]{1,0:T(8,128)(2,1)}, u32[]{:S(2)}) copy-start(bf16[256,1024]{1,0:T(8,128)(2,1)} %param.36) | copy-start | bytes 1572868
  888.7 407.3 %reduce-scatter.11.cloned.1.call-start = ((), (), s32[]{:S(2)}) async-start(), calls=%async_computation.11 | async-start | bytes 5570560 | tf_op jit(solution)/shard_map/reduce_scatter | solution.py:251
  992.6 2.4 copy-start.3
  1018.3 5.0 copy-start.13
  1023.3 3.8 copy-start.2
  1028.2 6.5 copy-start.60
  1091.9 2.4 copy-start.3
  1117.7 5.0 copy-start.13
  1122.7 3.8 copy-start.2
  1127.6 6.5 copy-start.60
  1186.0 3.4 copy-start.15
  1198.5 2.5 copy-start.21
  1204.1 4.5 copy-start.24
  1216.4 120.9 %all-reduce.8.cloned.1.call-start = ((), (), s32[]{:S(2)}) async-start(), calls=%async_computation.12 | async-start | bytes 131072 | tf_op jit(solution)/shard_map/psum | solution.py:17
  1216.4 19.6 %slice-start = ((s8[4456448]{0:T(1024)(128)(4,1)}), s8[4194304]{0:T(1024)(128)(4,1)S(1)}, s32[]{:S(2)}) async-start(s8[4456448]{0:T(1024)(128)(4,1)} %bitcast.261), calls=%async_computation.14 | async-start | bytes 8388608
  1226.4 9.7 copy-start.25
  1226.4 9.7 copy-start.26
  1226.4 9.7 slice-start.1
  1236.1 60.0 %copy-start.30 = (f32[544]{0:T(1024)S(1)}, f32[544]{0:T(1024)}, u32[]{:S(2)}) copy-start(f32[544]{0:T(1024)} %copy-done.29) | copy-start | bytes 6532
  1236.1 60.0 %copy-start.32 = (f32[544]{0:T(1024)S(1)}, f32[544]{0:T(1024)}, u32[]{:S(2)}) copy-start(f32[544]{0:T(1024)} %copy-done.31) | copy-start | bytes 6532
  1236.1 60.0 %copy-start.34 = (f32[1,1024]{1,0:T(1,128)S(1)}, f32[1,1024]{1,0:T(1,128)}, u32[]{:S(2)}) copy-start(f32[1,1024]{1,0:T(1,128)} %copy-done.33) | copy-start | bytes 12292
  1296.1 3.2 copy-start.6
  1296.1 3.2 copy-start.22
  1299.3 3.8 copy-start.39
  1304.6 216.5 %all-reduce.10.cloned.1.call-start = ((), (), s32[]{:S(2)}) async-start(), calls=%async_computation.13 | async-start | bytes 25296896 | tf_op jit(solution)/shard_map/psum | solution.py:272
  1337.3 15.7 %copy-start.51 = (f32[1024]{0:T(1024)S(1)}, f32[1024]{0:T(1024)}, u32[]{:S(2)}) copy-start(f32[1024]{0:T(1024)} %get-tuple-element.413) | copy-start | bytes 12292
  1521.1 3.6 copy-start.27
  1525.7 4.9 copy-start.23
  1525.7 7.6 copy-start.1
  (30 other events, 38.7 us)
Sparse Core Ops, SparseCore 0:
  15.0 87.2 all-gather.4
  190.4 151.0 reduce-scatter.4
  349.4 86.1 all-gather.6
  456.7 151.0 reduce-scatter.6
  615.3 86.1 all-gather.8
  726.1 151.0 reduce-scatter.8
  888.9 86.1 all-gather.10
  1216.5 79.5 reduce-scatter.10
  1304.8 32.4 all-reduce.7
  1343.3 177.8 all-reduce.9
